TPU v7x, 128 devices: a whole 4x4x4 slice. The times are simulated.
128 devices in a mesh: grp: 4 (over z_lo, core), dev: 32 (over y, z_hi, x).
Axes of the slice: x: 4, y: 4, z: 4 (z_hi: 2, z_lo: 2; z = z_hi * 2 + z_lo), core: 2. Of those that a mesh axis runs over, the one named last changes fastest.
Arguments:
- tokens: bfloat16 [16384, 2048], P(('grp', 'dev')), may hold values from -6 to 6
- queries: bfloat16 [16384, 2048], P(('grp', 'dev')), may hold values from -7.5 to 7.5
- suffix_keys: bfloat16 [16384, 2048], P(('grp', 'dev')), may hold values from -6 to 6
- suffix_values: bfloat16 [16384, 2048], P(('grp', 'dev')), may hold values from -6 to 6
- prefix_keys: bfloat16 [4, 1024, 2048], P('grp', 'dev'), may hold values from -6 to 6
- prefix_values: bfloat16 [4, 1024, 2048], P('grp', 'dev'), may hold values from -6 to 6
- out_weight: bfloat16 [2048, 2048], replicated, may hold values from -0.125 to 0.125
- norm_gain: float32 [2048], replicated, may hold values from 0.1 to 1.9
- routes: int32 [16384, 6], P(('grp', 'dev')), may hold values from 0 to 63, all different within a row; in each aligned block of 128 rows (0 to 127, 128 to 255, ...) at most 16 rows name the same one
- route_weights: float32 [16384, 6], P(('grp', 'dev')), may hold values from 0.05 to 0.5
- gate_up_weight: bfloat16 [128, 2048, 1408], P(('grp', 'dev')), may hold values from -0.125 to 0.125
- down_weight: bfloat16 [128, 704, 2048], P(('grp', 'dev')), may hold values from -0.15625 to 0.15625
Outputs:
- attended: bfloat16 [16384, 2048], P(('grp', 'dev'))
- routed: bfloat16 [16384, 2048], P(('grp', 'dev'))
Inputs may be any that keep to these rules, and one draw needn't show every extreme that they name: `routes`: each row names 6 different experts. Within the rows of one request (aligned blocks of 128 rows) no expert is named by more than 16 rows, and in some block one expert is named exactly 16 times.
All inputs are finite; a program needn't handle non-finite values.
Results may differ from a plain program's by a relative error of at most 0.019.
Values may be sent and summed in bfloat16 or wider, within the bound.
A program may use at most 128 MiB of HBM per device.

v0:
```python
import math
import jax
import jax.numpy as jnp
from jax import lax
from jax.sharding import PartitionSpec as P

HEADS = 16
HEAD_DIM = 128
TOP = 6


def half_expert(rows, gate_up, down_proj):
    hidden_units = down_proj.shape[0]
    projected = jnp.dot(rows, gate_up, preferred_element_type=jnp.float32)
    active = (jax.nn.silu(projected[:, :hidden_units]) * projected[:, hidden_units:]).astype(
        jnp.bfloat16
    )
    return jnp.dot(active, down_proj, preferred_element_type=jnp.float32).astype(jnp.bfloat16)


def on_device(
    tokens,
    queries,
    suffix_keys,
    suffix_values,
    prefix_keys,
    prefix_values,
    out_weight,
    norm_gain,
    routes,
    route_weights,
    gate_up_weight,
    down_weight,
):
    rows_here = tokens.shape[0]
    width = tokens.shape[1]
    divisor = math.sqrt(HEAD_DIM)
    query_heads = queries.reshape(rows_here, HEADS, HEAD_DIM)
    running_max = jnp.full((HEADS, rows_here), -jnp.inf, jnp.float32)
    denominator = jnp.zeros((HEADS, rows_here), jnp.float32)
    weighted = jnp.zeros((HEADS, rows_here, HEAD_DIM), jnp.float32)
    key_piece = lax.all_gather(prefix_keys[0], "dev", axis=0, tiled=True).reshape(
        -1, HEADS, HEAD_DIM
    )
    value_piece = lax.all_gather(prefix_values[0], "dev", axis=0, tiled=True).reshape(
        -1, HEADS, HEAD_DIM
    )
    scores = (
        jnp.einsum("rhd,khd->hrk", query_heads, key_piece, preferred_element_type=jnp.float32)
        / divisor
    )
    new_max = jnp.max(scores, axis=-1)
    shifted = jnp.exp(scores - new_max[..., None])
    factor = jnp.exp(running_max - new_max)
    denominator = denominator * factor + jnp.sum(shifted, axis=-1)
    weighted = weighted * factor[..., None] + jnp.einsum(
        "hrk,khd->hrd",
        shifted.astype(jnp.bfloat16),
        value_piece,
        preferred_element_type=jnp.float32,
    )
    causal = jnp.arange(rows_here)[:, None] >= jnp.arange(rows_here)[None, :]
    suffix_scores = (
        jnp.einsum(
            "rhd,khd->hrk",
            query_heads,
            suffix_keys.reshape(rows_here, HEADS, HEAD_DIM),
            preferred_element_type=jnp.float32,
        )
        / divisor
    )
    suffix_scores = jnp.where(causal[None], suffix_scores, -jnp.inf)
    suffix_max = jnp.max(suffix_scores, axis=-1)
    suffix_exp = jnp.exp(suffix_scores - suffix_max[..., None])
    suffix_sum = jnp.sum(suffix_exp, axis=-1)
    suffix_acc = jnp.einsum(
        "hrk,khd->hrd",
        suffix_exp.astype(jnp.bfloat16),
        suffix_values.reshape(rows_here, HEADS, HEAD_DIM),
        preferred_element_type=jnp.float32,
    )
    merged_max = jnp.maximum(new_max, suffix_max)
    prefix_scale = jnp.exp(new_max - merged_max)
    suffix_scale = jnp.exp(suffix_max - merged_max)
    mixed = (weighted * prefix_scale[..., None] + suffix_acc * suffix_scale[..., None]) / (
        denominator * prefix_scale + suffix_sum * suffix_scale
    )[..., None]
    heads_out = jnp.transpose(mixed, (1, 0, 2)).reshape(rows_here, width).astype(jnp.bfloat16)
    attended = jnp.dot(heads_out, out_weight, preferred_element_type=jnp.float32).astype(
        jnp.bfloat16
    )
    residual = tokens.astype(jnp.float32) + attended.astype(jnp.float32)
    mean_square = jnp.mean(residual * residual, axis=-1, keepdims=True)
    normed = (residual * lax.rsqrt(mean_square + 1e-06) * norm_gain).astype(jnp.bfloat16)
    groups = lax.axis_size("grp")
    members = lax.axis_size("dev")
    experts = groups * members // 2
    capacity = 4 * rows_here * TOP // (3 * experts)
    flat_routes = routes.reshape(-1)
    onehot = (flat_routes[:, None] == jnp.arange(experts, dtype=jnp.int32)[None, :]).astype(
        jnp.int32
    )
    ranking = jnp.sum(jnp.cumsum(onehot, axis=0) * onehot, axis=1) - 1
    slots = flat_routes * capacity + ranking
    owners = jnp.arange(rows_here * TOP, dtype=jnp.int32) // TOP
    outgoing = jnp.zeros((experts * capacity, width), jnp.bfloat16).at[slots].set(normed[owners])
    buffer = jnp.broadcast_to(
        outgoing.reshape(experts, 1, capacity, width), (experts, 2, capacity, width)
    ).reshape(2 * experts, capacity, width)
    received = lax.all_to_all(buffer, ("grp", "dev"), split_axis=0, concat_axis=0, tiled=True)
    partial_rows = half_expert(
        received.reshape(-1, width), gate_up_weight[0], down_weight[0]
    ).reshape(2 * experts, capacity, width)
    returned = lax.all_to_all(partial_rows, ("grp", "dev"), split_axis=0, concat_axis=0, tiled=True)
    halves = returned.reshape(experts, 2, capacity, width)
    expert_table = lax.optimization_barrier(
        (halves[:, 0].astype(jnp.float32) + halves[:, 1].astype(jnp.float32)).astype(jnp.bfloat16)
    ).reshape(experts * capacity, width)
    picked = expert_table[slots].astype(jnp.float32)
    weighted_rows = picked * route_weights.reshape(-1)[:, None]
    routed = jnp.sum(weighted_rows.reshape(rows_here, TOP, width), axis=1).astype(jnp.bfloat16)
    return (attended, routed)


def solution(mesh):
    return jax.shard_map(
        on_device,
        mesh=mesh,
        in_specs=(
            P(("grp", "dev"), None),
            P(("grp", "dev"), None),
            P(("grp", "dev"), None),
            P(("grp", "dev"), None),
            P("grp", "dev", None),
            P("grp", "dev", None),
            P(),
            P(),
            P(("grp", "dev"), None),
            P(("grp", "dev"), None),
            P(("grp", "dev"), None, None),
            P(("grp", "dev"), None, None),
        ),
        out_specs=(P(("grp", "dev"), None), P(("grp", "dev"), None)),
        check_vma=False,
    )
```

profile of v0, /device:TPU:1, one launch (start us, length us, event | category | flops | bytes accessed | tf_op | source)
XLA Modules:
  0.0 513.5 jit_solution(7477060815687853919)
XLA Ops:
  7.2 0.0 copy-start
  7.2 0.0 all-gather.5.cloned.1.call-start
  7.2 0.7 all-gather.5.cloned.1.call-update
  7.9 0.0 all-gather.7.cloned.1.call-start
  8.0 0.7 all-gather.7.cloned.1.call-update
  8.7 0.8 copy.47
  9.5 0.1 eq.29
  9.6 0.1 eq.25
  9.7 2.0 copy.55
  11.8 1.8 reduce-window.6
  13.6 0.3 slice_reduce_fusion
  13.9 0.7 broadcast_multiply_fusion
  14.6 0.1 copy.46
  14.7 0.1 mul.102
  14.9 0.1 fusion.42
  15.1 0.0 copy-start.6
  15.1 1.8 fusion.56
  16.9 0.0 copy-start.4
  16.9 1.0 copy-done.4
  17.9 0.2 fusion.30
  18.0 77.1 %all-gather.5.cloned.1.call-done = bf16[1,1024,2048]{2,1,0:T(8,128)(2,1)} async-done(((bf16[1,32,2048]{2,1,0:T(8,128)(2,1)}), bf16[1,1024,2048]{2,1,0:T(8,128)(2,1)}) %all-gather.5.cloned.1.call-update) | async-done | bytes 4194320 | tf_op jit(solution)/shard_map/all_gather | solution.py:42
  95.2 6.4 %copy.38 = bf16[1,1024,2048]{1,2,0:T(8,128)(2,1)} copy(bf16[1,1024,2048]{2,1,0:T(8,128)(2,1)} %all-gather.5.cloned.1.call-done) | data formatting | bytes 8388608 | tf_op jit(solution)/shard_map/all_gather | solution.py:42
  101.6 0.0 copy-done.6
  101.6 3.5 multiply_reduce_fusion.1
  105.1 0.0 copy-start.1
  105.1 3.2 copy-done.1
  108.3 1.8 fusion
  110.1 67.4 %all-gather.7.cloned.1.call-done = bf16[1,1024,2048]{2,1,0:T(8,128)(2,1)} async-done(((bf16[1,32,2048]{2,1,0:T(8,128)(2,1)}), bf16[1,1024,2048]{2,1,0:T(8,128)(2,1)}) %all-gather.7.cloned.1.call-update) | async-done | bytes 4194320 | tf_op jit(solution)/shard_map/all_gather | solution.py:45
  177.5 6.4 %copy.41 = bf16[1,1024,2048]{1,2,0:T(8,128)(2,1)} copy(bf16[1,1024,2048]{2,1,0:T(8,128)(2,1)} %all-gather.7.cloned.1.call-done) | data formatting | bytes 8388608 | tf_op jit(solution)/shard_map/all_gather | solution.py:45
  183.9 0.0 slice-start
  183.9 0.0 copy-start.5
  183.9 0.0 copy-start.7
  183.9 0.0 slice-start.1
  183.9 0.0 copy-start.2
  184.0 6.9 %fusion.26 = f32[128,16,128]{0,2,1:T(8,128)S(1)} fusion(bf16[1024,16,128]{0,2,1:T(8,128)(2,1)} %bitcast.121, f32[16,128,1024]{2,1,0:T(8,128)} %copy-done.1, f32[16,128]{1,0:T(8,128)S(1)} %get-tuple-element.6, f32[128,16]{0,1:T(8,128)S(1)} %get-tuple-element.4, f32[128,16]{0,1:T(8,128)S(1)} %get-tuple-element.5), kind=kOutput, calls=%fused_computation.34 | convolution fusion | flops 543686656 | bytes 13656064 | tf_op jit(solution)/shard_map/hrk,khd->hrd/dot_general | solution.py:56
  190.9 0.0 copy-done.5
  190.9 0.0 copy-done.7
  190.9 0.3 fusion.29
  191.2 0.0 slice-done
  191.3 0.3 slice-done.1
  191.6 0.0 copy-done.2
  191.6 0.0 copy-start.8
  191.6 1.4 multiply_reduce_fusion.2
  193.0 0.0 copy-start.3
  193.0 0.8 copy-done.3
  193.8 0.0 copy-done.8
  193.8 0.2 multiply_convert_fusion
  194.0 23.5 %scatter_custom_fusion = bf16[1024,2048]{1,0:T(8,128)(2,1)} fusion(s32[768]{0:T(1024)S(1)} %fusion.50, bf16[128,2048]{1,0:T(8,128)(2,1)S(1)} %multiply_convert_fusion, s32[1024]{0:T(1024)S(1)} %pad_clamp_fusion.1, bf16[]{:T(256)} %constant.17.clone.1), kind=kCustom, calls=%fused_computation.20 | custom fusion | bytes 4194306 | tf_op jit(solution)/shard_map/scatter | solution.py:106
  217.5 6.8 %broadcast_in_dim.28 = bf16[64,2,16,2048]{3,2,1,0:T(8,128)(2,1)} broadcast(bf16[64,16,2048]{2,1,0:T(8,128)(2,1)} %bitcast.120), dimensions={0,2,3} | broadcast | bytes 12582912 | tf_op jit(solution)/shard_map/broadcast_in_dim | solution.py:107
  224.3 105.2 %all_to_all.10 = bf16[128,16,2048]{2,1,0:T(8,128)(2,1)S(1)} all-to-all(bf16[128,16,2048]{2,1,0:T(8,128)(2,1)} %bitcast.117), channel_id=1, replica_groups=mesh['grp'=4,'dev'=32] {'grp','dev'}, dimensions={0} | all-to-all | bytes 16777216 | tf_op jit(solution)/shard_map/all_to_all | solution.py:110
  329.5 17.8 %fusion.3 = f32[2048,1408]{0,1:T(8,128)} fusion(bf16[2048,2048]{1,0:T(8,128)(2,1)S(1)} %bitcast.124, bf16[1,2048,1408]{2,1,0:T(8,128)(2,1)} %param.22), kind=kOutput, calls=%fused_computation.12 | convolution fusion | flops 11811160064 | bytes 25690112 | tf_op jit(solution)/shard_map/dot_general | solution.py:14
  347.3 0.0 copy-done
  347.3 13.5 %convolution_convert_fusion = bf16[2048,2048]{1,0:T(8,128)(2,1)} fusion(f32[2048,1408]{0,1:T(8,128)} %fusion.3, bf16[1,704,2048]{2,1,0:T(8,128)(2,1)S(1)} %copy-done), kind=kOutput, calls=%fused_computation.7 | convolution fusion | flops 5918425088 | bytes 22806528 | tf_op jit(solution)/shard_map/dot_general | solution.py:18
  360.8 0.0 copy-start.9
  360.8 7.9 %all-to-all-start.1 = ((bf16[128,16,2048]{2,1,0:T(8,128)(2,1)}), bf16[128,16,2048]{2,1,0:T(8,128)(2,1)}, u32[]{:S(2)}, u32[]{:S(2)}) async-start(bf16[128,16,2048]{2,1,0:T(8,128)(2,1)} %bitcast.123), calls=%async_computation.1 | async-start | bytes 16777216 | tf_op jit(solution)/shard_map/all_to_all | solution.py:114
  368.7 0.0 copy-done.9
  368.7 0.1 copy.52
  368.8 108.1 %all-to-all-done.1 = bf16[128,16,2048]{2,1,0:T(8,128)(2,1)} async-done(((bf16[128,16,2048]{2,1,0:T(8,128)(2,1)}), bf16[128,16,2048]{2,1,0:T(8,128)(2,1)}, u32[]{:S(2)}, u32[]{:S(2)}) %all-to-all-start.1) | async-done | bytes 8388640 | tf_op jit(solution)/shard_map/all_to_all | solution.py:114
  477.0 5.7 %fusion.7 = bf16[64,16,2048]{2,1,0:T(8,128)(2,1)} fusion(bf16[64,2,16,2048]{3,2,1,0:T(8,128)(2,1)} %bitcast.17), kind=kLoop, calls=%fused_computation.15 | loop fusion | flops 8388608 | bytes 12582912 | tf_op jit(solution)/shard_map/convert_element_type | solution.py:117
  482.7 9.8 %gather_fusion = bf16[768,2048]{1,0:T(8,128)(2,1)} fusion(bf16[1024,2048]{1,0:T(8,128)(2,1)} %bitcast.116, s32[1024]{0:T(1024)S(1)} %pad_clamp_fusion), kind=kCustom, calls=%fused_computation.1 | custom fusion | bytes 6294528 | tf_op jit(solution)/shard_map/gather | solution.py:119
  492.5 6.6 %reshape.210 = f32[128,6,2048]{2,1,0:T(8,128)} reshape(bf16[768,2048]{1,0:T(8,128)(2,1)} %gather_fusion) | data formatting | bytes 9437184 | tf_op jit(solution)/shard_map/convert_element_type | solution.py:119
  499.1 7.4 %multiply_reduce_fusion = bf16[128,2048]{1,0:T(8,128)(2,1)} fusion(f32[128,6,2048]{2,1,0:T(8,128)} %reshape.210, f32[128,6]{1,0:T(8,128)S(1)} %copy.52), kind=kLoop, calls=%fused_computation.3 | loop fusion | flops 2883584 | bytes 6818816 | tf_op jit(solution)/shard_map/reduce_sum | solution.py:121
  (11 shorter events, 0.1 us)
Async XLA Ops:
  7.2 340.1 %copy-start = (bf16[1,704,2048]{2,1,0:T(8,128)(2,1)S(1)}, bf16[1,704,2048]{2,1,0:T(8,128)(2,1)}, u32[]{:S(2)}) copy-start(bf16[1,704,2048]{2,1,0:T(8,128)(2,1)} %param.23) | copy-start | bytes 8650756
  7.2 88.0 %all-gather.5.cloned.1.call-start = ((), (), s32[]{:S(2)}) async-start(), calls=%async_computation.2 | async-start | bytes 4325376 | tf_op jit(solution)/shard_map/all_gather | solution.py:42
  7.9 169.6 %all-gather.7.cloned.1.call-start = ((), (), s32[]{:S(2)}) async-start(), calls=%async_computation.3 | async-start | bytes 4325376 | tf_op jit(solution)/shard_map/all_gather | solution.py:45
  15.1 86.5 %copy-start.6 = (bf16[128,2048]{1,0:T(8,128)(2,1)S(1)}, bf16[128,2048]{1,0:T(8,128)(2,1)}, u32[]{:S(2)}) copy-start(bf16[128,2048]{1,0:T(8,128)(2,1)} %param.13) | copy-start | bytes 1572868
  16.9 1.0 copy-start.4
  105.1 3.2 copy-start.1
  183.9 7.3 %slice-start = ((s8[8388608]{0:T(1024)(128)(4,1)}), s8[4194304]{0:T(1024)(128)(4,1)S(1)}, s32[]{:S(2)}) async-start(s8[8388608]{0:T(1024)(128)(4,1)} %bitcast.118), calls=%async_computation.4 | async-start | bytes 8388608
  183.9 7.0 %copy-start.5 = (f32[16,128,128]{1,2,0:T(8,128)S(1)}, f32[16,128,128]{1,2,0:T(8,128)}, u32[]{:S(2)}) copy-start(f32[16,128,128]{1,2,0:T(8,128)} %copy-done.4) | copy-start | bytes 3145732
  183.9 7.0 %copy-start.7 = (bf16[128,2048]{0,1:T(8,128)(2,1)S(1)}, bf16[128,2048]{0,1:T(8,128)(2,1)}, u32[]{:S(2)}) copy-start(bf16[128,2048]{0,1:T(8,128)(2,1)} %copy.55) | copy-start | bytes 1572868
  183.9 7.7 %slice-start.1 = ((s8[8388608]{0:T(1024)(128)(4,1)}), s8[4194304]{0:T(1024)(128)(4,1)S(1)}, s32[]{:S(2)}) async-start(s8[8388608]{0:T(1024)(128)(4,1)} %bitcast.118), calls=%async_computation.5 | async-start | bytes 8388608
  183.9 7.6 %copy-start.2 = (bf16[128,2048]{1,0:T(8,128)(2,1)S(1)}, bf16[128,2048]{1,0:T(8,128)(2,1)}, u32[]{:S(2)}) copy-start(bf16[128,2048]{1,0:T(8,128)(2,1)} %param.12) | copy-start | bytes 1572868
  191.6 2.2 copy-start.8
  193.0 0.8 copy-start.3
  360.8 7.9 %copy-start.9 = (f32[128,6]{0,1:T(8,128)S(1)}, f32[128,6]{0,1:T(8,128)}, u32[]{:S(2)}) copy-start(f32[128,6]{0,1:T(8,128)} %param.21) | copy-start | bytes 9220
  360.8 116.2 %all-to-all-start.1 = ((bf16[128,16,2048]{2,1,0:T(8,128)(2,1)}), bf16[128,16,2048]{2,1,0:T(8,128)(2,1)}, u32[]{:S(2)}, u32[]{:S(2)}) async-start(bf16[128,16,2048]{2,1,0:T(8,128)(2,1)} %bitcast.123), calls=%async_computation.1 | async-start | bytes 16777216 | tf_op jit(solution)/shard_map/all_to_all | solution.py:114
Sparse Core Ops, SparseCore 0:
  11.0 84.1 all-gather.4
  98.2 79.3 all-gather.6
where the time goes:
time: 521 us; the launch traced here: 514 us
  waiting for transfers between devices  254 us (49%)
  blocking collectives  105 us (20%)
  local copies, waits for them, and re-layouts  68.5 us (13%)
  matrix products  45.2 us (9%)
  other arithmetic  18 us (3%)
  between operations  14.5 us (3%)
  starting transfers between devices  7.99 us (2%)
    all_to_all x1, waiting for transfers between devices, on_device(): lax.all_to_all(partial_rows, ('grp', 'dev'), split_axis=0, concat_axis=0,...  108 us
    all_to_all x1, blocking collectives, on_device(): lax.all_to_all(buffer, ('grp', 'dev'), split_axis=0, concat_axis=0, tiled...  105 us
    all_gather x1, waiting for transfers between devices, on_device(): lax.all_gather(prefix_keys[0], 'dev', axis=0, tiled=True)  77.1 us
    all_gather x1, waiting for transfers between devices, on_device(): lax.all_gather(prefix_values[0], 'dev', axis=0, tiled=True)  67.4 us
    scatter x1, local copies, waits for them, and re-layouts, on_device(): jnp.zeros((experts * capacity, width), jnp.bfloat16).at[slots]  23.5 us
    dot_general x1, matrix products, half_expert(): projected = jnp.dot(rows, gate_up, preferred_element_type=jnp.float32)  17.8 us
    dot_general x1, matrix products, half_expert(): jnp.dot(active, down_proj, preferred_element_type=jnp.float32)  13.5 us
  transfers between devices with their start and end apart: 3, of which 3 were waited for; matrix products, arithmetic and copies ran while one was open for 4% of the time, Pallas kernels for 0%

commit v1 on v0

--- a/solution.py
+++ b/solution.py
@@ -42,9 +42,9 @@
     key_piece = lax.all_gather(prefix_keys[0], "dev", axis=0, tiled=True).reshape(
         -1, HEADS, HEAD_DIM
     )
-    value_piece = lax.all_gather(prefix_values[0], "dev", axis=0, tiled=True).reshape(
-        -1, HEADS, HEAD_DIM
-    )
+    value_piece = jnp.concatenate(
+        lax.all_to_all(jnp.stack([prefix_values[0]] * lax.axis_size("dev")), "dev", 0, 0), axis=0
+    ).reshape(-1, HEADS, HEAD_DIM)
     scores = (
         jnp.einsum("rhd,khd->hrk", query_heads, key_piece, preferred_element_type=jnp.float32)
         / divisor

time: 521 us -> 497 us (0.954)
  waiting for transfers between devices: 254 us -> 210 us
  starting transfers between devices: 7.99 us -> 19.7 us
    all_gather x1 -> x0, waiting for transfers between devices: 67.4 us -> none  [on_device(): lax.all_gather(prefix_values[0], 'dev', axis=0, tiled=True)]
    all_to_all x0 -> x1, waiting for transfers between devices: none -> 45.6 us  [on_device(): lax.all_to_all(jnp.stack([prefix_values[0]] * lax.axis_size('dev')), 'dev...]
    all_gather x1, waiting for transfers between devices: 77.1 us -> 55.7 us  [on_device(): lax.all_gather(prefix_keys[0], 'dev', axis=0, tiled=True)]
    all_to_all x0 -> x1, starting transfers between devices: none -> 11.3 us  [on_device(): lax.all_to_all(jnp.stack([prefix_values[0]] * lax.axis_size('dev')), 'dev...]
    scatter x1, local copies, waits for them, and re-layouts: 23.5 us -> 30.9 us  [on_device(): jnp.zeros((experts * capacity, width), jnp.bfloat16).at[slots]]
    all_gather x1 -> x0, local copies, waits for them, and re-layouts: 6.41 us -> none  [on_device(): lax.all_gather(prefix_values[0], 'dev', axis=0, tiled=True)]
  transfers between devices with their start and end apart: 3 -> 3, of which waited for: 3 -> 3; matrix products, arithmetic and copies ran while one was open for 4% -> 3% of each run, Pallas kernels for 0% -> 0%
where the time goes in v1:
time: 497 us; the launch traced here: 489 us
  waiting for transfers between devices  210 us (42%)
  blocking collectives  105 us (21%)
  local copies, waits for them, and re-layouts  73.7 us (15%)
  matrix products  47.8 us (10%)
  starting transfers between devices  19.7 us (4%)
  other arithmetic  18.2 us (4%)
  between operations  14.5 us (3%)
    all_to_all x1, waiting for transfers between devices, on_device(): lax.all_to_all(partial_rows, ('grp', 'dev'), split_axis=0, concat_axis=0,...  108 us
    all_to_all x1, blocking collectives, on_device(): lax.all_to_all(buffer, ('grp', 'dev'), split_axis=0, concat_axis=0, tiled...  105 us
    all_gather x1, waiting for transfers between devices, on_device(): lax.all_gather(prefix_keys[0], 'dev', axis=0, tiled=True)  55.7 us
    all_to_all x1, waiting for transfers between devices, on_device(): lax.all_to_all(jnp.stack([prefix_values[0]] * lax.axis_size('dev')), 'dev...  45.6 us
    scatter x1, local copies, waits for them, and re-layouts, on_device(): jnp.zeros((experts * capacity, width), jnp.bfloat16).at[slots]  30.9 us
    dot_general x1, matrix products, half_expert(): projected = jnp.dot(rows, gate_up, preferred_element_type=jnp.float32)  17.8 us
    dot_general x1, matrix products, half_expert(): jnp.dot(active, down_proj, preferred_element_type=jnp.float32)  13.5 us
    all_to_all x1, starting transfers between devices, on_device(): lax.all_to_all(jnp.stack([prefix_values[0]] * lax.axis_size('dev')), 'dev...  11.3 us
  transfers between devices with their start and end apart: 3, of which 3 were waited for; matrix products, arithmetic and copies ran while one was open for 3% of the time, Pallas kernels for 0%

profile of v1, /device:TPU:1, one launch (start us, length us, event | category | flops | bytes accessed | tf_op | source)
XLA Modules:
  0.0 488.9 jit_solution(12124428347087472853)
XLA Ops:
  7.2 0.0 copy-start
  7.2 0.0 all-gather.3.cloned.1.call-start
  7.2 0.7 all-gather.3.cloned.1.call-update
  7.9 0.0 copy-start.7
  7.9 0.0 copy-start.6
  7.9 3.5 stack.3
  11.4 11.3 %all-to-all-start = ((bf16[32,32,2048]{2,1,0:T(8,128)(2,1)}), bf16[32,32,2048]{2,1,0:T(8,128)(2,1)}, u32[]{:S(2)}, u32[]{:S(2)}) async-start(bf16[32,32,2048]{2,1,0:T(8,128)(2,1)} %stack.3), calls=%async_computation | async-start | bytes 8388608 | tf_op jit(solution)/shard_map/all_to_all | solution.py:46
  22.8 0.0 copy-done.7
  22.8 0.1 copy.47
  22.9 0.1 eq.29
  23.0 0.1 eq.25
  23.2 0.0 copy-done.6
  23.2 1.0 copy.55
  24.2 1.8 reduce-window.6
  26.0 0.3 slice_reduce_fusion
  26.3 0.1 copy.46
  26.4 0.1 mul.102
  26.6 0.1 fusion.49
  26.8 1.7 fusion.63
  28.5 0.0 copy-start.4
  28.5 1.0 copy-done.4
  29.6 0.2 fusion.37
  29.7 45.6 %all-to-all-done = bf16[32,32,2048]{2,1,0:T(8,128)(2,1)} async-done(((bf16[32,32,2048]{2,1,0:T(8,128)(2,1)}), bf16[32,32,2048]{2,1,0:T(8,128)(2,1)}, u32[]{:S(2)}, u32[]{:S(2)}) %all-to-all-start) | async-done | bytes 4194336 | tf_op jit(solution)/shard_map/all_to_all | solution.py:46
  75.4 5.6 %copy.61 = bf16[128,8,16,128]{3,2,1,0:T(8,128)(2,1)} copy(bf16[128,8,16,128]{3,1,2,0:T(8,128)(2,1)} %bitcast.29) | data formatting | bytes 8388608
  80.9 0.0 copy-start.5
  80.9 55.7 %all-gather.3.cloned.1.call-done = bf16[1,1024,2048]{2,1,0:T(8,128)(2,1)} async-done(((bf16[1,32,2048]{2,1,0:T(8,128)(2,1)}), bf16[1,1024,2048]{2,1,0:T(8,128)(2,1)}) %all-gather.3.cloned.1.call-update) | async-done | bytes 4194320 | tf_op jit(solution)/shard_map/all_gather | solution.py:42
  136.6 6.4 %copy.38 = bf16[1,1024,2048]{1,2,0:T(8,128)(2,1)} copy(bf16[1,1024,2048]{2,1,0:T(8,128)(2,1)} %all-gather.3.cloned.1.call-done) | data formatting | bytes 8388608 | tf_op jit(solution)/shard_map/all_gather | solution.py:42
  143.0 0.0 copy-done.5
  143.0 3.5 multiply_reduce_fusion.1
  146.5 0.0 copy-start.1
  146.5 1.9 fusion
  148.4 0.3 copy-done.1
  148.7 0.0 copy-start.2
  148.7 4.4 fusion.31
  153.1 2.0 fusion.36
  155.2 0.0 copy-done.2
  155.2 0.0 copy-start.8
  155.2 4.8 multiply_reduce_fusion.2
  160.0 0.0 copy-start.3
  160.0 0.8 copy-done.3
  160.8 0.0 copy-done.8
  160.8 1.0 multiply_convert_fusion
  161.8 30.9 %scatter_custom_fusion = bf16[1024,2048]{1,0:T(8,128)(2,1)} fusion(s32[768]{0:T(1024)S(1)} %fusion.57, bf16[128,2048]{1,0:T(8,128)(2,1)} %multiply_convert_fusion, s32[1024]{0:T(1024)S(1)} %pad_clamp_fusion.1, bf16[]{:T(256)} %constant.17.clone.1), kind=kCustom, calls=%fused_computation.21 | custom fusion | bytes 4194816 | tf_op jit(solution)/shard_map/scatter | solution.py:106
  192.7 6.8 %broadcast_in_dim.28 = bf16[64,2,16,2048]{3,2,1,0:T(8,128)(2,1)} broadcast(bf16[64,16,2048]{2,1,0:T(8,128)(2,1)} %bitcast.120), dimensions={0,2,3} | broadcast | bytes 12582912 | tf_op jit(solution)/shard_map/broadcast_in_dim | solution.py:107
  199.5 105.0 %all_to_all.15 = bf16[128,16,2048]{2,1,0:T(8,128)(2,1)S(1)} all-to-all(bf16[128,16,2048]{2,1,0:T(8,128)(2,1)} %bitcast.119), channel_id=1, replica_groups=mesh['grp'=4,'dev'=32] {'grp','dev'}, dimensions={0} | all-to-all | bytes 16777216 | tf_op jit(solution)/shard_map/all_to_all | solution.py:110
  304.4 17.8 %fusion.3 = f32[2048,1408]{0,1:T(8,128)} fusion(bf16[2048,2048]{1,0:T(8,128)(2,1)S(1)} %bitcast.123, bf16[1,2048,1408]{2,1,0:T(8,128)(2,1)} %param.22), kind=kOutput, calls=%fused_computation.12 | convolution fusion | flops 11811160064 | bytes 25690112 | tf_op jit(solution)/shard_map/dot_general | solution.py:14
  322.2 0.0 copy-done
  322.2 13.5 %convolution_convert_fusion = bf16[2048,2048]{1,0:T(8,128)(2,1)} fusion(f32[2048,1408]{0,1:T(8,128)} %fusion.3, bf16[1,704,2048]{2,1,0:T(8,128)(2,1)S(1)} %copy-done), kind=kOutput, calls=%fused_computation.7 | convolution fusion | flops 5918425088 | bytes 22806528 | tf_op jit(solution)/shard_map/dot_general | solution.py:18
  335.8 0.0 copy-start.9
  335.8 8.3 %all-to-all-start.2 = ((bf16[128,16,2048]{2,1,0:T(8,128)(2,1)}), bf16[128,16,2048]{2,1,0:T(8,128)(2,1)}, u32[]{:S(2)}, u32[]{:S(2)}) async-start(bf16[128,16,2048]{2,1,0:T(8,128)(2,1)} %bitcast.122), calls=%async_computation.2 | async-start | bytes 16777216 | tf_op jit(solution)/shard_map/all_to_all | solution.py:114
  344.1 0.0 copy-done.9
  344.1 0.1 copy.52
  344.2 108.1 %all-to-all-done.2 = bf16[128,16,2048]{2,1,0:T(8,128)(2,1)} async-done(((bf16[128,16,2048]{2,1,0:T(8,128)(2,1)}), bf16[128,16,2048]{2,1,0:T(8,128)(2,1)}, u32[]{:S(2)}, u32[]{:S(2)}) %all-to-all-start.2) | async-done | bytes 8388640 | tf_op jit(solution)/shard_map/all_to_all | solution.py:114
  452.4 5.7 %fusion.7 = bf16[64,16,2048]{2,1,0:T(8,128)(2,1)} fusion(bf16[64,2,16,2048]{3,2,1,0:T(8,128)(2,1)} %bitcast.17), kind=kLoop, calls=%fused_computation.15 | loop fusion | flops 8388608 | bytes 12582912 | tf_op jit(solution)/shard_map/convert_element_type | solution.py:117
  458.1 9.8 %gather_fusion = bf16[768,2048]{1,0:T(8,128)(2,1)} fusion(bf16[1024,2048]{1,0:T(8,128)(2,1)} %bitcast.118, s32[1024]{0:T(1024)S(1)} %pad_clamp_fusion), kind=kCustom, calls=%fused_computation.1 | custom fusion | bytes 6294528 | tf_op jit(solution)/shard_map/gather | solution.py:119
  467.9 6.6 %reshape.207 = f32[128,6,2048]{2,1,0:T(8,128)} reshape(bf16[768,2048]{1,0:T(8,128)(2,1)} %gather_fusion) | data formatting | bytes 9437184 | tf_op jit(solution)/shard_map/convert_element_type | solution.py:119
  474.4 7.4 %multiply_reduce_fusion = bf16[128,2048]{1,0:T(8,128)(2,1)} fusion(f32[128,6,2048]{2,1,0:T(8,128)} %reshape.207, f32[128,6]{1,0:T(8,128)S(1)} %copy.52), kind=kLoop, calls=%fused_computation.3 | loop fusion | flops 2883584 | bytes 6818816 | tf_op jit(solution)/shard_map/reduce_sum | solution.py:121
  (11 shorter events, 0.1 us)
Async XLA Ops:
  7.2 315.1 %copy-start = (bf16[1,704,2048]{2,1,0:T(8,128)(2,1)S(1)}, bf16[1,704,2048]{2,1,0:T(8,128)(2,1)}, u32[]{:S(2)}) copy-start(bf16[1,704,2048]{2,1,0:T(8,128)(2,1)} %param.23) | copy-start | bytes 8650756
  7.2 129.4 %all-gather.3.cloned.1.call-start = ((), (), s32[]{:S(2)}) async-start(), calls=%async_computation.3 | async-start | bytes 4325376 | tf_op jit(solution)/shard_map/all_gather | solution.py:42
  7.9 14.8 %copy-start.7 = (s32[128,6]{0,1:T(8,128)S(1)}, s32[128,6]{0,1:T(8,128)}, u32[]{:S(2)}) copy-start(s32[128,6]{0,1:T(8,128)} %param.20) | copy-start | bytes 9220
  7.9 15.2 %copy-start.6 = (bf16[128,2048]{1,0:T(8,128)(2,1)S(1)}, bf16[128,2048]{1,0:T(8,128)(2,1)}, u32[]{:S(2)}) copy-start(bf16[128,2048]{1,0:T(8,128)(2,1)} %param.15) | copy-start | bytes 1572868
  11.4 63.9 %all-to-all-start = ((bf16[32,32,2048]{2,1,0:T(8,128)(2,1)}), bf16[32,32,2048]{2,1,0:T(8,128)(2,1)}, u32[]{:S(2)}, u32[]{:S(2)}) async-start(bf16[32,32,2048]{2,1,0:T(8,128)(2,1)} %stack.3), calls=%async_computation | async-start | bytes 8388608 | tf_op jit(solution)/shard_map/all_to_all | solution.py:46
  28.5 1.1 copy-start.4
  80.9 62.1 %copy-start.5 = (bf16[128,2048]{1,0:T(8,128)(2,1)S(1)}, bf16[128,2048]{1,0:T(8,128)(2,1)}, u32[]{:S(2)}) copy-start(bf16[128,2048]{1,0:T(8,128)(2,1)} %param.13) | copy-start | bytes 1572868
  146.5 2.2 copy-start.1
  148.7 6.5 %copy-start.2 = (bf16[128,2048]{1,0:T(8,128)(2,1)S(1)}, bf16[128,2048]{1,0:T(8,128)(2,1)}, u32[]{:S(2)}) copy-start(bf16[128,2048]{1,0:T(8,128)(2,1)} %param.12) | copy-start | bytes 1572868
  155.2 5.6 %copy-start.8 = (f32[2048]{0:T(1024)S(1)}, f32[2048]{0:T(1024)}, u32[]{:S(2)}) copy-start(f32[2048]{0:T(1024)} %param.19) | copy-start | bytes 24580
  160.0 0.8 copy-start.3
  335.8 8.3 %copy-start.9 = (f32[128,6]{0,1:T(8,128)S(1)}, f32[128,6]{0,1:T(8,128)}, u32[]{:S(2)}) copy-start(f32[128,6]{0,1:T(8,128)} %param.21) | copy-start | bytes 9220
  335.8 116.6 %all-to-all-start.2 = ((bf16[128,16,2048]{2,1,0:T(8,128)(2,1)}), bf16[128,16,2048]{2,1,0:T(8,128)(2,1)}, u32[]{:S(2)}, u32[]{:S(2)}) async-start(bf16[128,16,2048]{2,1,0:T(8,128)(2,1)} %bitcast.122), calls=%async_computation.2 | async-start | bytes 16777216 | tf_op jit(solution)/shard_map/all_to_all | solution.py:114
Sparse Core Ops, SparseCore 0:
  11.0 125.5 all-gather.2
